TPU v7x, 32 devices: a whole 2x2x4 slice. The times are simulated.
32 devices in a mesh: dp: 8 (over y, x, core), seq: 4 (over z).
Axes of the slice: x: 2, y: 2, z: 4, core: 2. Of those that a mesh axis runs over, the one named last changes fastest.
Arguments:
- layer_input: bfloat16 [8, 1024, 2048], P('dp', 'seq'), may hold values from -6 to 6
- segments: int32 [8, 1024], P('dp'), may hold values from 0 to 3, never falling along the last dimension, each value on 1 to 512 neighbouring positions
- w_query: bfloat16 [2048, 2048], P(('dp', 'seq')), may hold values from -0.125 to 0.125
- w_key: bfloat16 [2048, 2048], P(('dp', 'seq')), may hold values from -0.125 to 0.125
- w_value: bfloat16 [2048, 2048], P(('dp', 'seq')), may hold values from -0.125 to 0.125
- w_output: bfloat16 [2048, 2048], P(('dp', 'seq')), may hold values from -0.125 to 0.125
- w_gate: bfloat16 [2048, 8192], P(('dp', 'seq')), may hold values from -0.125 to 0.125
- w_up: bfloat16 [2048, 8192], P(('dp', 'seq')), may hold values from -0.125 to 0.125
- w_down: bfloat16 [8192, 2048], P(None, ('dp', 'seq')), may hold values from -0.0625 to 0.0625
- query_gain: float32 [2048], replicated, may hold values from 0.1 to 1.9
- key_gain: float32 [2048], replicated, may hold values from 0.1 to 1.9
- attn_gain: float32 [2048], replicated, may hold values from 0.1 to 1.9
- ff_gain: float32 [2048], replicated, may hold values from 0.1 to 1.9
- cotangent: bfloat16 [8, 1024, 2048], P('dp', 'seq'), may hold values from -6 to 6
Outputs:
- activation: bfloat16 [8, 1024, 2048], P('dp', 'seq')
- input_grad: bfloat16 [8, 1024, 2048], P('dp', 'seq')
- grad_query: float32 [2048, 2048], P(('dp', 'seq'))
- grad_key: float32 [2048, 2048], P(('dp', 'seq'))
- grad_value: float32 [2048, 2048], P(('dp', 'seq'))
- grad_output: float32 [2048, 2048], P(('dp', 'seq'))
- grad_gate: float32 [2048, 8192], P(('dp', 'seq'))
- grad_up: float32 [2048, 8192], P(('dp', 'seq'))
- grad_down: float32 [8192, 2048], P(None, ('dp', 'seq'))
- grad_query_gain: float32 [2048], P(('dp', 'seq'))
- grad_key_gain: float32 [2048], P(('dp', 'seq'))
- grad_attn_gain: float32 [2048], P(('dp', 'seq'))
- grad_ff_gain: float32 [2048], P(('dp', 'seq'))
Inputs may be any that keep to these rules, and one draw needn't show every extreme that they name: `segments`: segment numbers never fall along a row, and a document holds at most half of 1024 tokens.
All inputs are finite; a program needn't handle non-finite values.
Results may differ from a plain program's by a relative error of at most 0.017.
Values may be sent and summed in bfloat16 or wider, within the bound.
No kernel may reach another device: no remote copies, remote signals or barrier semaphores. Data moves between devices by JAX's collectives and lax.ppermute only.
A program may use at most 384 MiB of HBM per device.

v0:
```python
import jax
import jax.numpy as jnp
from jax import lax
from jax.sharding import PartitionSpec as P

HD = 128
EPSILON = 1e-06
ROPE_BASE = 500000.0
MASKED = -1e30


def rms_norm(values, gain_vec):
    factor = lax.rsqrt(jnp.mean(values * values, axis=-1, keepdims=True) + EPSILON)
    return values * factor * gain_vec


def rope_tables(positions):
    half_dim = HD // 2
    frequency = jnp.power(
        jnp.float32(ROPE_BASE), -jnp.arange(half_dim, dtype=jnp.float32) * (2.0 / HD)
    )
    angles = positions[:, None] * frequency[None, :]
    angles = jnp.concatenate([angles, angles], axis=-1)
    return (jnp.cos(angles), jnp.sin(angles))


def rotate(values, cosine_table, sine_table):
    shaped = values.reshape(values.shape[:-1] + (values.shape[-1] // HD, HD))
    first_half = shaped[..., : HD // 2]
    second = shaped[..., HD // 2 :]
    turned = jnp.concatenate([-second, first_half], axis=-1)
    rotated = shaped * cosine_table[:, None, :] + turned * sine_table[:, None, :]
    return rotated.reshape(values.shape)


def project(left, weight):
    return jnp.dot(left, weight, preferred_element_type=jnp.float32)


def back_project(grad_in, weight):
    return lax.dot_general(
        grad_in, weight, (((grad_in.ndim - 1,), (1,)), ((), ())), preferred_element_type=jnp.float32
    )


def rows_product(left, right):
    return lax.dot_general(
        left, right, (((0,), (0,)), ((), ())), preferred_element_type=jnp.float32
    )


def block_mask(segments, row_start, block_rows):
    seq_length = segments.shape[1]
    query_pos = row_start + jnp.arange(block_rows, dtype=jnp.int32)
    query_seg = lax.dynamic_slice_in_dim(segments, row_start, block_rows, 1)
    key_pos = jnp.arange(seq_length, dtype=jnp.int32)
    causal = key_pos[None, None, :] <= query_pos[None, :, None]
    return causal & (segments[:, None, :] == query_seg[:, :, None])


def block_scores(query_block, key_heads, segments, row_start, block_rows):
    score_scale = HD ** (-0.5)
    scores = (
        jnp.einsum("rqhd,rkhd->rhqk", query_block, key_heads, preferred_element_type=jnp.float32)
        * score_scale
    )
    allowed = block_mask(segments, row_start, block_rows)
    return jnp.where(allowed[:, None], scores, MASKED)


def attend(query_all, key_all, value_all, segments):
    row_count, seq_length, local_width = query_all.shape
    head_count = local_width // HD
    block_rows = min(512, seq_length)
    block_count = seq_length // block_rows
    query_split = query_all.reshape(row_count, block_count, block_rows, head_count, HD)
    key_heads = key_all.reshape(row_count, seq_length, head_count, HD)
    value_heads = value_all.reshape(row_count, seq_length, head_count, HD)

    def one_block(block_index):
        query_block = lax.dynamic_index_in_dim(query_split, block_index, 1, keepdims=False)
        scores = block_scores(
            query_block, key_heads, segments, block_index * block_rows, block_rows
        )
        top_score = jnp.max(scores, axis=-1, keepdims=True)
        exp_scores = jnp.exp(scores - top_score)
        row_total = jnp.sum(exp_scores, axis=-1, keepdims=True)
        probs_full = exp_scores / row_total
        log_total = top_score + jnp.log(row_total)
        mixed = jnp.einsum(
            "rhqk,rkhd->rqhd",
            probs_full.astype(jnp.bfloat16),
            value_heads,
            preferred_element_type=jnp.float32,
        )
        return (mixed.astype(jnp.bfloat16), log_total[..., 0])

    mixed_blocks, log_totals = lax.map(one_block, jnp.arange(block_count, dtype=jnp.int32))
    mixed_all = jnp.moveaxis(mixed_blocks, 0, 1).reshape(row_count, seq_length, local_width)
    return (mixed_all, log_totals)


def attend_back(query_all, key_all, value_all, grad_mixed, log_totals, segments):
    row_count, seq_length, local_width = query_all.shape
    head_count = local_width // HD
    block_rows = min(512, seq_length)
    block_count = seq_length // block_rows
    score_scale = HD ** (-0.5)
    query_split = query_all.reshape(row_count, block_count, block_rows, head_count, HD)
    grad_split = grad_mixed.reshape(row_count, block_count, block_rows, head_count, HD)
    key_heads = key_all.reshape(row_count, seq_length, head_count, HD)
    value_heads = value_all.reshape(row_count, seq_length, head_count, HD)

    def one_block(totals, step_item):
        block_index, log_total = step_item
        grad_keys, grad_values = totals
        query_block = lax.dynamic_index_in_dim(query_split, block_index, 1, keepdims=False)
        grad_block = lax.dynamic_index_in_dim(grad_split, block_index, 1, keepdims=False)
        scores = block_scores(
            query_block, key_heads, segments, block_index * block_rows, block_rows
        )
        probs_full = jnp.exp(scores - log_total[..., None])
        grad_probs = jnp.einsum(
            "rqhd,rkhd->rhqk", grad_block, value_heads, preferred_element_type=jnp.float32
        )
        grad_values = grad_values + jnp.einsum(
            "rhqk,rqhd->rkhd",
            probs_full.astype(jnp.bfloat16),
            grad_block,
            preferred_element_type=jnp.float32,
        )
        inner = jnp.sum(probs_full * grad_probs, axis=-1, keepdims=True)
        grad_scores = (probs_full * (grad_probs - inner)).astype(jnp.bfloat16)
        grad_query = (
            jnp.einsum(
                "rhqk,rkhd->rqhd", grad_scores, key_heads, preferred_element_type=jnp.float32
            )
            * score_scale
        )
        grad_keys = (
            grad_keys
            + jnp.einsum(
                "rhqk,rqhd->rkhd", grad_scores, query_block, preferred_element_type=jnp.float32
            )
            * score_scale
        )
        return ((grad_keys, grad_values), grad_query.astype(jnp.bfloat16))

    zeros_heads = jnp.zeros((row_count, seq_length, head_count, HD), jnp.float32)
    (grad_keys, grad_values), grad_queries = lax.scan(
        one_block,
        (zeros_heads, zeros_heads),
        (jnp.arange(block_count, dtype=jnp.int32), log_totals),
    )
    grad_queries = jnp.moveaxis(grad_queries, 0, 1).reshape(row_count, seq_length, local_width)
    grad_keys = grad_keys.reshape(row_count, seq_length, local_width).astype(jnp.bfloat16)
    grad_values = grad_values.reshape(row_count, seq_length, local_width).astype(jnp.bfloat16)
    return (grad_queries, grad_keys, grad_values)


def silu_mix(gate_in, up_in):
    return jax.nn.silu(gate_in) * up_in


def shards(
    layer_input,
    segments,
    w_query,
    w_key,
    w_value,
    w_output,
    w_gate,
    w_up,
    w_down,
    query_gain,
    key_gain,
    attn_gain,
    ff_gain,
    cotangent,
):
    row_count, local_len, model_width = layer_input.shape
    offset = lax.axis_index("seq") * local_len
    positions = (offset + jnp.arange(local_len, dtype=jnp.int32)).astype(jnp.float32)
    cosine_table, sine_table = rope_tables(positions)

    def front(values, gain_vec):
        return rotate(rms_norm(values, gain_vec), cosine_table, sine_table)

    wq_all, wk_all, wv_all, wo_all = (
        lax.all_gather(w_query, ("dp", "seq"), axis=0, tiled=True),
        lax.all_gather(w_key, ("dp", "seq"), axis=0, tiled=True),
        lax.all_gather(w_value, ("dp", "seq"), axis=0, tiled=True),
        lax.all_gather(w_output, ("dp", "seq"), axis=0, tiled=True),
    )
    q_proj = project(layer_input, wq_all)
    k_proj = project(layer_input, wk_all)
    v_proj = project(layer_input, wv_all)
    q_rot, query_back = jax.vjp(front, q_proj, query_gain)
    k_rot, key_back = jax.vjp(front, k_proj, key_gain)
    q_low = q_rot.astype(jnp.bfloat16)
    k_low = k_rot.astype(jnp.bfloat16)
    v_low = v_proj.astype(jnp.bfloat16)
    q_heads, k_heads, v_heads = (
        lax.all_to_all(q_low, "seq", split_axis=2, concat_axis=1, tiled=True),
        lax.all_to_all(k_low, "seq", split_axis=2, concat_axis=1, tiled=True),
        lax.all_to_all(v_low, "seq", split_axis=2, concat_axis=1, tiled=True),
    )
    mixed_heads, log_totals = attend(q_heads, k_heads, v_heads, segments)
    mixed_local = lax.all_to_all(mixed_heads, "seq", split_axis=1, concat_axis=2, tiled=True)
    attn_out = project(mixed_local, wo_all)
    attn_normed, attn_back = jax.vjp(rms_norm, attn_out, attn_gain)
    residual = layer_input.astype(jnp.float32) + attn_normed
    residual_low = residual.astype(jnp.bfloat16)
    grad_top = cotangent.astype(jnp.float32)
    gate_part, up_part, down_part = (
        lax.all_to_all(w_gate, "seq", split_axis=1, concat_axis=0, tiled=True),
        lax.all_to_all(w_up, "seq", split_axis=1, concat_axis=0, tiled=True),
        lax.all_to_all(w_down.T, "seq", split_axis=1, concat_axis=0, tiled=True),
    )
    wg_blk, wu_blk, wd_blk = (
        lax.all_gather(gate_part, "dp", axis=0, tiled=True),
        lax.all_gather(up_part, "dp", axis=0, tiled=True),
        lax.all_gather(down_part, "dp", axis=0, tiled=True),
    )
    resid_full, cot_full = (
        lax.all_gather(residual_low, "seq", axis=1, tiled=True),
        lax.all_gather(cotangent, "seq", axis=1, tiled=True),
    )
    gate_act = project(resid_full, wg_blk)
    up_act = project(resid_full, wu_blk)
    hidden_low = silu_mix(gate_act, up_act).astype(jnp.bfloat16)
    ff_full = lax.psum(back_project(hidden_low, wd_blk).astype(jnp.bfloat16), "seq").astype(
        jnp.float32
    )
    ff_own = lax.dynamic_slice_in_dim(ff_full, offset, local_len, 1)
    ff_normed, ff_back = jax.vjp(rms_norm, ff_own, ff_gain)
    activation = (residual + ff_normed).astype(jnp.bfloat16)
    _, grad_ffg = ff_back(grad_top)
    _, full_back = jax.vjp(rms_norm, ff_full, ff_gain)
    grad_ff32, _ = full_back(cot_full.astype(jnp.float32))
    grad_ff = grad_ff32.astype(jnp.bfloat16)
    grad_hidden = project(grad_ff, wd_blk)
    _, mix_back = jax.vjp(silu_mix, gate_act, up_act)
    grad_gate32, grad_up32 = mix_back(grad_hidden)
    grad_gate_low = grad_gate32.astype(jnp.bfloat16)
    grad_up_low = grad_up32.astype(jnp.bfloat16)
    partial_resid = back_project(grad_gate_low, wg_blk) + back_project(grad_up_low, wu_blk)
    grad_resid = grad_top + lax.psum_scatter(partial_resid, "seq", scatter_dimension=1, tiled=True)
    residual_flat = resid_full.reshape(-1, model_width)
    grad_ff_flat = grad_ff.reshape(-1, model_width)
    hidden_flat = hidden_low.reshape(-1, hidden_low.shape[-1])
    grad_gate_flat = grad_gate_low.reshape(-1, hidden_low.shape[-1])
    grad_up_flat = grad_up_low.reshape(-1, hidden_low.shape[-1])
    block_width = hidden_low.shape[-1]
    mlp_blocks = lax.psum_scatter(
        jnp.concatenate(
            [
                rows_product(residual_flat, grad_gate_flat),
                rows_product(residual_flat, grad_up_flat),
                rows_product(grad_ff_flat, hidden_flat),
            ],
            axis=1,
        ).astype(jnp.bfloat16),
        "dp",
        scatter_dimension=0,
        tiled=True,
    ).astype(jnp.float32)
    grad_gate, grad_up, grad_down_rows = (
        lax.all_to_all(
            mlp_blocks[:, :block_width].astype(jnp.bfloat16),
            "seq",
            split_axis=0,
            concat_axis=1,
            tiled=True,
        ).astype(jnp.float32),
        lax.all_to_all(
            mlp_blocks[:, block_width : 2 * block_width].astype(jnp.bfloat16),
            "seq",
            split_axis=0,
            concat_axis=1,
            tiled=True,
        ).astype(jnp.float32),
        lax.all_to_all(
            mlp_blocks[:, 2 * block_width :].astype(jnp.bfloat16),
            "seq",
            split_axis=0,
            concat_axis=1,
            tiled=True,
        ).astype(jnp.float32),
    )
    grad_down = grad_down_rows.T
    grad_attn32, grad_attng = attn_back(grad_resid)
    grad_attn = grad_attn32.astype(jnp.bfloat16)
    grad_mixed = back_project(grad_attn, wo_all).astype(jnp.bfloat16)
    grad_mixed_heads = lax.all_to_all(grad_mixed, "seq", split_axis=2, concat_axis=1, tiled=True)
    grad_qh, grad_kh, grad_vh = attend_back(
        q_heads, k_heads, v_heads, grad_mixed_heads, log_totals, segments
    )
    grad_q_rot, grad_k_rot, grad_value_low = (
        lax.all_to_all(grad_qh, "seq", split_axis=1, concat_axis=2, tiled=True),
        lax.all_to_all(grad_kh, "seq", split_axis=1, concat_axis=2, tiled=True),
        lax.all_to_all(grad_vh, "seq", split_axis=1, concat_axis=2, tiled=True),
    )
    grad_q32, grad_qg = query_back(grad_q_rot.astype(jnp.float32))
    grad_k32, grad_kg = key_back(grad_k_rot.astype(jnp.float32))
    grad_query_low = grad_q32.astype(jnp.bfloat16)
    grad_key_low = grad_k32.astype(jnp.bfloat16)
    input_grad = (
        grad_resid
        + back_project(grad_query_low, wq_all)
        + back_project(grad_key_low, wk_all)
        + back_project(grad_value_low, wv_all)
    ).astype(jnp.bfloat16)
    input_flat = layer_input.reshape(-1, model_width)
    mixed_flat = mixed_local.reshape(-1, model_width)
    grad_query_flat = grad_query_low.reshape(-1, model_width)
    grad_key_flat = grad_key_low.reshape(-1, model_width)
    grad_value_flat = grad_value_low.reshape(-1, model_width)
    grad_attn_flat = grad_attn.reshape(-1, model_width)
    attn_part = lax.psum_scatter(
        jnp.concatenate(
            [
                rows_product(input_flat, grad_query_flat),
                rows_product(input_flat, grad_key_flat),
                rows_product(input_flat, grad_value_flat),
                rows_product(mixed_flat, grad_attn_flat),
            ],
            axis=1,
        ),
        ("dp", "seq"),
        scatter_dimension=0,
        tiled=True,
    )
    gain_stack = jnp.stack([grad_qg, grad_kg, grad_attng, grad_ffg])
    gain_shares = lax.psum_scatter(gain_stack, ("dp", "seq"), scatter_dimension=1, tiled=True)
    grad_query = attn_part[:, :model_width]
    grad_key = attn_part[:, model_width : 2 * model_width]
    grad_value = attn_part[:, 2 * model_width : 3 * model_width]
    grad_output = attn_part[:, 3 * model_width :]
    return (
        activation,
        input_grad,
        grad_query,
        grad_key,
        grad_value,
        grad_output,
        grad_gate,
        grad_up,
        grad_down,
        gain_shares[0],
        gain_shares[1],
        gain_shares[2],
        gain_shares[3],
    )


def solution(mesh):
    placed = (
        P("dp", "seq", None),
        P("dp", None),
        P(("dp", "seq"), None),
        P(("dp", "seq"), None),
        P(("dp", "seq"), None),
        P(("dp", "seq"), None),
        P(("dp", "seq"), None),
        P(("dp", "seq"), None),
        P(None, ("dp", "seq")),
        P(),
        P(),
        P(),
        P(),
        P("dp", "seq", None),
    )
    return jax.shard_map(
        shards,
        mesh=mesh,
        in_specs=placed,
        out_specs=(
            P("dp", "seq", None),
            P("dp", "seq", None),
            P(("dp", "seq"), None),
            P(("dp", "seq"), None),
            P(("dp", "seq"), None),
            P(("dp", "seq"), None),
            P(("dp", "seq"), None),
            P(("dp", "seq"), None),
            P(None, ("dp", "seq")),
            P(("dp", "seq")),
            P(("dp", "seq")),
            P(("dp", "seq")),
            P(("dp", "seq")),
        ),
        check_vma=False,
    )
```

profile of v0, /device:TPU:0, one launch (start us, length us, event | category | flops | bytes accessed | tf_op | source)
XLA Modules:
  0.0 3019.1 jit_solution(3999838460059790055)
XLA Ops:
  19.4 30.5 %all-to-all-done.4 = bf16[64,4,2048]{2,0,1:T(8,128)(2,1)S(1)} async-done(((bf16[64,4,2048]{2,0,1:T(8,128)(2,1)}), bf16[64,4,2048]{2,0,1:T(8,128)(2,1)S(1)}, u32[]{:S(2)}, u32[]{:S(2)}) %all-to-all-start.4) | async-done | bytes 1048608 | tf_op jit(solution)/shard_map/all_to_all | solution.py:216
  50.9 51.7 %all-gather.14.cloned.1.call-done = bf16[2048,2048]{1,0:T(8,128)(2,1)} async-done(((bf16[64,2048]{1,0:T(8,128)(2,1)}), bf16[2048,2048]{1,0:T(8,128)(2,1)}) %all-gather.14.cloned.1.call-update) | async-done | bytes 8388624 | tf_op jit(solution)/shard_map/all_gather | solution.py:192
  114.5 11.6 reduce.28
  134.0 58.4 %all-gather.12.cloned.1.call-done = bf16[2048,2048]{1,0:T(8,128)(2,1)} async-done(((bf16[64,2048]{1,0:T(8,128)(2,1)}), bf16[2048,2048]{1,0:T(8,128)(2,1)}) %all-gather.12.cloned.1.call-update) | async-done | bytes 8388624 | tf_op jit(solution)/shard_map/all_gather | solution.py:191
  201.6 69.9 %all-gather.10.cloned.1.call-done = bf16[2048,2048]{1,0:T(8,128)(2,1)} async-done(((bf16[64,2048]{1,0:T(8,128)(2,1)}), bf16[2048,2048]{1,0:T(8,128)(2,1)}) %all-gather.10.cloned.1.call-update) | async-done | bytes 8388624 | tf_op jit(solution)/shard_map/all_gather | solution.py:190
  292.6 11.6 reduce.27
  313.6 10.6 reduce.26
  325.9 32.2 %all-to-all-done.1 = bf16[4,2,65536]{2,1,0:T(2,128)(2,1)} async-done(((bf16[4,2,65536]{2,1,0:T(2,128)(2,1)}), bf16[4,2,65536]{2,1,0:T(2,128)(2,1)}, u32[]{:S(2)}, u32[]{:S(2)}) %all-to-all-start.1) | async-done | bytes 1048608 | tf_op jit(solution)/shard_map/all_to_all | solution.py:205
  372.0 15.0 all-to-all-done
  399.5 25.0 while.27
  431.7 9.0 reduce.29
  444.4 28.9 all_to_all.204
  485.9 55.2 %all_to_all.205 = bf16[64,4,2048]{2,0,1:T(8,128)(2,1)} all-to-all(bf16[64,4,2048]{2,0,1:T(8,128)(2,1)S(1)} %bitcast.443), channel_id=1, replica_groups=mesh['dp'=8,'seq'=4] {'seq'}, dimensions={1} | all-to-all | bytes 2097152 | tf_op jit(solution)/shard_map/all_to_all | solution.py:217
  541.3 52.8 %all_to_all.206 = bf16[64,4,2048]{2,0,1:T(8,128)(2,1)} all-to-all(bf16[64,4,2048]{2,0,1:T(8,128)(2,1)S(1)} %bitcast.444), channel_id=1, replica_groups=mesh['dp'=8,'seq'=4] {'seq'}, dimensions={1} | all-to-all | bytes 2097152 | tf_op jit(solution)/shard_map/all_to_all | solution.py:218
  594.9 9.1 all-gather.18.cloned.1.call-done
  604.0 14.7 fusion.49
  618.7 39.7 %all-gather.22.cloned.1.call-done = bf16[2048,2048]{1,0:T(8,128)(2,1)} async-done(((bf16[256,2048]{1,0:T(8,128)(2,1)}), bf16[2048,2048]{1,0:T(8,128)(2,1)}) %all-gather.22.cloned.1.call-update) | async-done | bytes 8388624 | tf_op jit(solution)/shard_map/all_gather | solution.py:222
  658.4 17.0 multiply_convert_fusion.2
  675.4 39.3 %all-gather.24.cloned.1.call-done = bf16[2048,2048]{1,0:T(8,128)(2,1)} async-done(((bf16[256,2048]{1,0:T(8,128)(2,1)}), bf16[2048,2048]{1,0:T(8,128)(2,1)}) %all-gather.24.cloned.1.call-update) | async-done | bytes 8388624 | tf_op jit(solution)/shard_map/all_gather | solution.py:223
  714.8 14.0 convert_bitcast_fusion
  728.8 68.3 %all-gather.26.cloned.1.call-done = bf16[1,1024,2048]{2,1,0:T(8,128)(2,1)} async-done(((bf16[1,256,2048]{2,1,0:T(8,128)(2,1)}), bf16[1,1024,2048]{2,1,0:T(8,128)(2,1)}) %all-gather.26.cloned.1.call-update) | async-done | bytes 4194320 | tf_op jit(solution)/shard_map/all_gather | solution.py:227
  797.1 155.8 %all-reduce.6.cloned.1.call-done = bf16[1,1024,2048]{2,1,0:T(8,128)(2,1)} async-done(((bf16[1,1024,2048]{2,1,0:T(8,128)(2,1)}), bf16[1,1024,2048]{2,1,0:T(8,128)(2,1)}) %all-reduce.6.cloned.1.call-update) | async-done | bytes 4194320 | tf_op jit(solution)/shard_map/psum | solution.py:232
  958.0 23.0 multiply_convert_fusion.1
  981.0 12.7 fusion.91
  993.7 13.8 add_bitcast_fusion
  1007.5 14.5 convolution_convert_fusion.1
  1022.1 11.2 convolution_convert_fusion.2
  1033.3 13.6 convolution_convert_fusion
  1046.9 18.1 pad_maximum_fusion.1
  1072.3 78.8 %reduce-scatter.9.cloned.1.call-done = f32[1,256,2048]{2,1,0:T(8,128)} async-done(((f32[1,1024,2048]{2,1,0:T(8,128)}), f32[1,256,2048]{2,1,0:T(8,128)}) %reduce-scatter.9.cloned.1.call-update) | async-done | bytes 2097168 | tf_op jit(solution)/shard_map/reduce_scatter | solution.py:248
  1167.5 10.8 reduce.30
  1184.4 25.7 all-to-all-done.7
  1221.0 43.4 %while.28 = (s32[]{:T(128)}, f32[1,1024,4,128]{1,3,2,0:T(8,128)S(1)}, f32[1,1024,4,128]{1,3,2,0:T(8,128)}, bf16[2,1,512,4,128]{4,3,2,0,1:T(4,128)(2,1)}, s32[2]{...) while((s32[]{:T(128)}, ...), condition=%wide.region_15.16_spmd.clone, body=%wide.region_13.15_spmd.clone.sunk | while | flops 2720528896 | bytes 98113936 | solution.py:150
  1271.5 8.0 reduce.32
  1297.3 14.4 all-to-all-done.8
  1319.7 8.1 reduce.31
  1331.6 9.7 all-to-all-done.9
  1345.0 8.2 fusion.92
  1396.4 8.1 convolution_bitcast_fusion.2
  1404.5 8.2 convolution_bitcast_fusion.1
  1412.7 8.1 convolution_bitcast_fusion
  1420.9 45.1 %pad_maximum_fusion = f32[2048,8192]{0,1:T(8,128)} fusion(f32[2048,2048]{0,1:T(8,128)} %fusion.92, f32[2048,2048]{0,1:T(8,128)} %convolution_bitcast_fusion, f32[2048,2048]{0,1:T(8,128)} %convolution_bitcast_fusion.1, f32[2048,2048]{0,1:T(8,128)} %convolution_bitcast_fusion.2), kind=kLoop, calls=%fused_computation.57 | loop fusion | flops 50331648 | bytes 134217728 | tf_op jit(solution)/shard_map/concatenate | solution.py:321
  1466.0 61.3 %copy.230 = f32[2048,8192]{1,0:T(8,128)} copy(f32[2048,8192]{0,1:T(8,128)} %pad_maximum_fusion) | data formatting | bytes 134217728
  1539.3 24.2 all-to-all-done.13
  1584.8 37.2 %all-to-all-done.12 = bf16[4,64,2048]{2,1,0:T(8,128)(2,1)} async-done(((bf16[4,64,2048]{2,1,0:T(8,128)(2,1)}), bf16[4,64,2048]{2,1,0:T(8,128)(2,1)}, u32[]{:S(2)}, u32[]{:S(2)}) %all-to-all-start.12) | async-done | bytes 1048608 | tf_op jit(solution)/shard_map/all_to_all | solution.py:276
  1626.2 8.4 fusion.54
  1643.8 37.9 %all-to-all-done.11 = bf16[4,64,2048]{2,1,0:T(8,128)(2,1)} async-done(((bf16[4,64,2048]{2,1,0:T(8,128)(2,1)}), bf16[4,64,2048]{2,1,0:T(8,128)(2,1)}, u32[]{:S(2)}, u32[]{:S(2)}) %all-to-all-start.11) | async-done | bytes 1048608 | tf_op jit(solution)/shard_map/all_to_all | solution.py:269
  1684.6 1324.6 %reduce-scatter.13.cloned.1.call-done = f32[64,8192]{1,0:T(8,128)} async-done(((f32[2048,8192]{1,0:T(8,128)}), f32[64,8192]{1,0:T(8,128)}) %reduce-scatter.13.cloned.1.call-update) | async-done | bytes 2097168
  (383 shorter events, 363.7 us)
Async XLA Ops:
  7.2 95.5 %copy-start.13 = (bf16[1,256,2048]{2,1,0:T(8,128)(2,1)S(1)}, bf16[1,256,2048]{2,1,0:T(8,128)(2,1)}, u32[]{:S(2)}) copy-start(bf16[1,256,2048]{2,1,0:T(8,128)(2,1)} %param.18) | copy-start | bytes 3145732
  7.2 95.5 %all-gather.14.cloned.1.call-start = ((), (), s32[]{:S(2)}) async-start(), calls=%async_computation.20 | async-start | bytes 8650752 | tf_op jit(solution)/shard_map/all_gather | solution.py:192
  7.9 184.5 %all-gather.12.cloned.1.call-start = ((), (), s32[]{:S(2)}) async-start(), calls=%async_computation.19 | async-start | bytes 8650752 | tf_op jit(solution)/shard_map/all_gather | solution.py:191
  8.7 262.8 %all-gather.10.cloned.1.call-start = ((), (), s32[]{:S(2)}) async-start(), calls=%async_computation.18 | async-start | bytes 8650752 | tf_op jit(solution)/shard_map/all_gather | solution.py:190
  9.4 467.4 %all-gather.16.cloned.1.call-start = ((), (), s32[]{:S(2)}) async-start(), calls=%async_computation.21 | async-start | bytes 8650752 | tf_op jit(solution)/shard_map/all_gather | solution.py:193
  12.3 37.6 %all-to-all-start.4 = ((bf16[64,4,2048]{2,0,1:T(8,128)(2,1)}), bf16[64,4,2048]{2,0,1:T(8,128)(2,1)S(1)}, u32[]{:S(2)}, u32[]{:S(2)}) async-start(bf16[64,4,2048]{2,0,1:T(8,128)(2,1)} %bitcast.345), calls=%async_computation.4 | async-start | bytes 2097152 | tf_op jit(solution)/shard_map/all_to_all | solution.py:216
  18.6 576.3 %all-gather.20.cloned.1.call-start = ((), (), s32[]{:S(2)}) async-start(), calls=%async_computation.23 | async-start | bytes 9437184 | tf_op jit(solution)/shard_map/all_gather | solution.py:221
  19.2 83.5 %copy-start.42 = (f32[256,128]{0,1:T(8,128)}, f32[256,128]{0,1:T(8,128)S(1)}, u32[]{:S(2)}) copy-start(f32[256,128]{0,1:T(8,128)S(1)} %get-tuple-element.404) | copy-start | bytes 393220
  19.2 83.5 %copy-start.44 = (f32[256,128]{0,1:T(8,128)}, f32[256,128]{0,1:T(8,128)S(1)}, u32[]{:S(2)}) copy-start(f32[256,128]{0,1:T(8,128)S(1)} %get-tuple-element.405) | copy-start | bytes 393220
  129.5 178.2 %all-to-all-start.2 = ((bf16[4,2,65536]{2,1,0:T(2,128)(2,1)}), bf16[4,2,65536]{2,1,0:T(2,128)(2,1)}, u32[]{:S(2)}, u32[]{:S(2)}) async-start(bf16[4,2,65536]{2,1,0:T(2,128)(2,1)} %reshape.886), calls=%async_computation.2 | async-start | bytes 2097152 | tf_op jit(solution)/shard_map/all_to_all | solution.py:206
  134.0 64.3 %copy-start.52 = (f32[2048]{0:T(1024)S(1)}, f32[2048]{0:T(1024)}, u32[]{:S(2)}) copy-start(f32[2048]{0:T(1024)} %param.28) | copy-start | bytes 24580
  198.2 84.3 %copy-start.6 = (f32[256,2048]{1,0:T(8,128)}, f32[256,2048]{1,0:T(8,128)S(1)}, u32[]{:S(2)}) copy-start(f32[256,2048]{1,0:T(8,128)S(1)} %get-tuple-element.413) | copy-start | bytes 6291460
  198.2 84.3 %copy-start.61 = (f32[256]{0:T(256)}, f32[256]{0:T(256)S(1)}, u32[]{:S(2)}) copy-start(f32[256]{0:T(256)S(1)} %fusion.83) | copy-start | bytes 3076
  201.6 75.7 %copy-start.54 = (f32[2048]{0:T(1024)S(1)}, f32[2048]{0:T(1024)}, u32[]{:S(2)}) copy-start(f32[2048]{0:T(1024)} %param.27) | copy-start | bytes 24580
  307.7 50.4 %all-to-all-start.1 = ((bf16[4,2,65536]{2,1,0:T(2,128)(2,1)}), bf16[4,2,65536]{2,1,0:T(2,128)(2,1)}, u32[]{:S(2)}, u32[]{:S(2)}) async-start(bf16[4,2,65536]{2,1,0:T(2,128)(2,1)} %reshape.884), calls=%async_computation.1 | async-start | bytes 2097152 | tf_op jit(solution)/shard_map/all_to_all | solution.py:205
  358.1 28.9 all-to-all-start
  362.4 241.6 %all-gather.18.cloned.1.call-start = ((), (), s32[]{:S(2)}) async-start(), calls=%async_computation.22 | async-start | bytes 5242880 | tf_op jit(solution)/shard_map/all_gather | solution.py:226
  424.4 19.9 copy-start
  424.4 19.9 copy-start.2
  424.4 19.9 copy-start.4
  424.4 20.0 copy-start.56
  485.7 55.4 %copy-start.47 = (bf16[8192,64]{0,1:T(8,128)(2,1)S(1)}, bf16[8192,64]{0,1:T(8,128)(2,1)}, u32[]{:S(2)}) copy-start(bf16[8192,64]{0,1:T(8,128)(2,1)} %param.26) | copy-start | bytes 3145732
  485.7 172.7 %all-gather.22.cloned.1.call-start = ((), (), s32[]{:S(2)}) async-start(), calls=%async_computation.24 | async-start | bytes 9437184 | tf_op jit(solution)/shard_map/all_gather | solution.py:222
  541.1 173.7 %all-gather.24.cloned.1.call-start = ((), (), s32[]{:S(2)}) async-start(), calls=%async_computation.25 | async-start | bytes 9437184 | tf_op jit(solution)/shard_map/all_gather | solution.py:223
  594.1 203.0 %all-gather.26.cloned.1.call-start = ((), (), s32[]{:S(2)}) async-start(), calls=%async_computation.27 | async-start | bytes 5242880 | tf_op jit(solution)/shard_map/all_gather | solution.py:227
  594.8 358.1 %all-reduce.6.cloned.1.call-start = ((), (), s32[]{:S(2)}) async-start(), calls=%async_computation.26 | async-start | bytes 8388608 | tf_op jit(solution)/shard_map/psum | solution.py:232
  728.7 224.2 %copy-start.60 = (f32[2048]{0:T(1024)S(1)}, f32[2048]{0:T(1024)}, u32[]{:S(2)}) copy-start(f32[2048]{0:T(1024)} %param.30) | copy-start | bytes 24580
  728.8 422.3 %reduce-scatter.9.cloned.1.call-start = ((), (), s32[]{:S(2)}) async-start(), calls=%async_computation.28 | async-start | bytes 10485760 | tf_op jit(solution)/shard_map/reduce_scatter | solution.py:248
  1007.5 519.9 %reduce-scatter.11.cloned.1.call-start = ((), (), s32[]{:S(2)}) async-start(), calls=%async_computation.29 | async-start | bytes 28311552 | tf_op jit(solution)/shard_map/reduce_scatter | solution.py:255
  1007.5 14.5 copy-start.73
  1065.0 86.1 %copy-start.12 = (f32[256,2048]{1,0:T(8,128)S(1)}, f32[256,2048]{1,0:T(8,128)}, u32[]{:S(2)}) copy-start(f32[256,2048]{1,0:T(8,128)} %copy-done.11) | copy-start | bytes 6291460
  1065.0 86.1 %copy-start.15 = (bf16[1,256,2048]{2,1,0:T(8,128)(2,1)S(1)}, bf16[1,256,2048]{2,1,0:T(8,128)(2,1)}, u32[]{:S(2)}) copy-start(bf16[1,256,2048]{2,1,0:T(8,128)(2,1)} %param.18) | copy-start | bytes 3145732
  1065.0 86.1 %copy-start.51 = (f32[2048]{0:T(1024)S(1)}, f32[2048]{0:T(1024)}, u32[]{:S(2)}) copy-start(f32[2048]{0:T(1024)} %param.29) | copy-start | bytes 24580
  1065.0 86.1 %copy-start.66 = (f32[256]{0:T(256)S(1)}, f32[256]{0:T(256)}, u32[]{:S(2)}) copy-start(f32[256]{0:T(256)} %copy-done.65) | copy-start | bytes 3076
  1072.3 85.2 %copy-start.68 = (f32[256]{0:T(256)S(1)}, f32[256]{0:T(256)}, u32[]{:S(2)}) copy-start(f32[256]{0:T(256)} %copy-done.67) | copy-start | bytes 3076
  1180.0 30.2 %all-to-all-start.7 = ((bf16[4,2,65536]{2,1,0:T(2,128)(2,1)}), bf16[4,2,65536]{2,1,0:T(2,128)(2,1)S(1)}, u32[]{:S(2)}, u32[]{:S(2)}) async-start(bf16[4,2,65536]{2,1,0:T(2,128)(2,1)} %reshape.890), calls=%async_computation.8 | async-start | bytes 2097152 | tf_op jit(solution)/shard_map/all_to_all | solution.py:295
  1281.5 30.1 all-to-all-start.8
  1311.7 29.7 all-to-all-start.9
  1319.7 25.3 copy-start.24
  1327.8 17.2 copy-start.41
  1341.4 28.7 all-to-all-start.10
  1344.9 289.8 %reduce-scatter.15.cloned.1.call-start = ((), (), s32[]{:S(2)}) async-start(), calls=%async_computation.31 | async-start | bytes 1081344
  1420.9 1588.4 %reduce-scatter.13.cloned.1.call-start = ((), (), s32[]{:S(2)}) async-start(), calls=%async_computation.30 | async-start | bytes 69206016
  1532.2 31.3 %all-to-all-start.13 = ((bf16[4,64,2048]{2,1,0:T(8,128)(2,1)}), bf16[4,64,2048]{2,1,0:T(8,128)(2,1)S(1)}, u32[]{:S(2)}, u32[]{:S(2)}) async-start(bf16[4,64,2048]{2,1,0:T(8,128)(2,1)} %bitcast.442), calls=%async_computation.15 | async-start | bytes 2097152 | tf_op jit(solution)/shard_map/all_to_all | solution.py:283
  1563.5 58.4 %all-to-all-start.12 = ((bf16[4,64,2048]{2,1,0:T(8,128)(2,1)}), bf16[4,64,2048]{2,1,0:T(8,128)(2,1)}, u32[]{:S(2)}, u32[]{:S(2)}) async-start(bf16[4,64,2048]{2,1,0:T(8,128)(2,1)} %bitcast.441), calls=%async_computation.14 | async-start | bytes 2097152 | tf_op jit(solution)/shard_map/all_to_all | solution.py:276
  1582.3 43.9 %copy-start.26 = (bf16[1,256,2048]{2,1,0:T(8,128)(2,1)S(1)}, bf16[1,256,2048]{2,1,0:T(8,128)(2,1)}, u32[]{:S(2)}) copy-start(bf16[1,256,2048]{2,1,0:T(8,128)(2,1)} %param.31) | copy-start | bytes 3145732
  1582.3 43.9 %copy-start.28 = (f32[1,256,2048]{2,1,0:T(8,128)S(1)}, f32[1,256,2048]{2,1,0:T(8,128)}, u32[]{:S(2)}) copy-start(f32[1,256,2048]{2,1,0:T(8,128)} %reduce-scatter.9.cloned.1.call-done) | copy-start | bytes 6291460
  1622.0 59.8 %all-to-all-start.11 = ((bf16[4,64,2048]{2,1,0:T(8,128)(2,1)}), bf16[4,64,2048]{2,1,0:T(8,128)(2,1)}, u32[]{:S(2)}, u32[]{:S(2)}) async-start(bf16[4,64,2048]{2,1,0:T(8,128)(2,1)} %bitcast.438), calls=%async_computation.13 | async-start | bytes 2097152 | tf_op jit(solution)/shard_map/all_to_all | solution.py:269
  (60 other events, 282.3 us)
Sparse Core Ops, SparseCore 0:
  11.0 91.6 all-gather.13
  105.6 86.8 all-gather.11
  195.4 76.0 all-gather.9
  274.3 89.3 all-gather.15
  365.4 52.4 all-gather.19
  485.8 118.1 all-gather.17
  605.9 52.5 all-gather.21
  660.3 54.3 all-gather.23
  716.3 80.7 all-gather.25
  799.3 153.5 all-reduce.5
  1007.6 143.4 reduce-scatter.8
  1155.0 157.5 reduce-scatter.10
  1421.0 137.4 reduce-scatter.14
  1560.7 1448.5 reduce-scatter.12
where the time goes:
time: 3030 us; the launch traced here: 3020 us
  waiting for transfers between devices  2130 us (70%)
  matrix products  256 us (8%)
  local copies, waits for them, and re-layouts  223 us (7%)
  other arithmetic  199 us (7%)
  blocking collectives  137 us (5%)
  starting transfers between devices  50.6 us (2%)
    unnamed x16, waiting for transfers between devices  1330 us
    psum x1, waiting for transfers between devices, shards(): lax.psum(back_project(hidden_low, wd_blk).astype(jnp.bfloat16), 'seq')  156 us
    unnamed x173, local copies, waits for them, and re-layouts  131 us
    unnamed x15, other arithmetic  81.6 us
    dot_general x7, matrix products, project(): return jnp.dot(left, weight, preferred_element_type=jnp.float32)  79.2 us
    reduce_scatter x1, waiting for transfers between devices, shards(): lax.psum_scatter(partial_resid, 'seq', scatter_dimension=1, tiled=True)  78.8 us
    dot_general x7, matrix products, rows_product(): lax.dot_general(left, right, (((0,), (0,)), ((), ())), preferred_element_...  71.9 us
    dot_general x7, matrix products, back_project(): lax.dot_general(grad_in, weight, (((grad_in.ndim - 1,), (1,)), ((), ())),...  69.9 us
  transfers between devices with their start and end apart: 25, of which 20 were waited for; matrix products, arithmetic and copies ran while one was open for 20% of the time, Pallas kernels for 0%

commit v1 on v0

--- a/solution.py
+++ b/solution.py
@@ -229,9 +229,9 @@
     gate_act = project(resid_full, wg_blk)
     up_act = project(resid_full, wu_blk)
     hidden_low = silu_mix(gate_act, up_act).astype(jnp.bfloat16)
-    ff_full = lax.psum(back_project(hidden_low, wd_blk).astype(jnp.bfloat16), "seq").astype(
-        jnp.float32
-    )
+    ff_full = jnp.sum(
+        lax.all_gather(back_project(hidden_low, wd_blk).astype(jnp.bfloat16), "seq"), axis=0
+    ).astype(jnp.float32)
     ff_own = lax.dynamic_slice_in_dim(ff_full, offset, local_len, 1)
     ff_normed, ff_back = jax.vjp(rms_norm, ff_own, ff_gain)
     activation = (residual + ff_normed).astype(jnp.bfloat16)

time: 3030 us -> 3170 us (1.046)
  waiting for transfers between devices: 2130 us -> 2250 us
    all_gather x0 -> x1, waiting for transfers between devices: none -> 286 us  [shards(): lax.all_gather(back_project(hidden_low, wd_blk).astype(jnp.bfloat16), 'seq')]
    psum x1 -> x0, waiting for transfers between devices: 156 us -> none  [shards(): lax.psum(back_project(hidden_low, wd_blk).astype(jnp.bfloat16), 'seq')]
  transfers between devices with their start and end apart: 25 -> 25, of which waited for: 20 -> 20; matrix products, arithmetic and copies ran while one was open for 20% -> 19% of each run, Pallas kernels for 0% -> 0%
where the time goes in v1:
time: 3170 us; the launch traced here: 3160 us
  waiting for transfers between devices  2250 us (71%)
  matrix products  257 us (8%)
  local copies, waits for them, and re-layouts  223 us (7%)
  other arithmetic  215 us (7%)
  blocking collectives  137 us (4%)
  starting transfers between devices  50.9 us (2%)
    unnamed x16, waiting for transfers between devices  1330 us
    all_gather x1, waiting for transfers between devices, shards(): lax.all_gather(back_project(hidden_low, wd_blk).astype(jnp.bfloat16), 'seq')  286 us
    unnamed x173, local copies, waits for them, and re-layouts  131 us
    unnamed x15, other arithmetic  81.6 us
    dot_general x7, matrix products, project(): return jnp.dot(left, weight, preferred_element_type=jnp.float32)  78.9 us
    reduce_scatter x1, waiting for transfers between devices, shards(): lax.psum_scatter(partial_resid, 'seq', scatter_dimension=1, tiled=True)  78.4 us
    dot_general x7, matrix products, rows_product(): lax.dot_general(left, right, (((0,), (0,)), ((), ())), preferred_element_...  71.8 us
    dot_general x7, matrix products, back_project(): lax.dot_general(grad_in, weight, (((grad_in.ndim - 1,), (1,)), ((), ())),...  70.4 us
  transfers between devices with their start and end apart: 25, of which 20 were waited for; matrix products, arithmetic and copies ran while one was open for 19% of the time, Pallas kernels for 0%

profile of v1, /device:TPU:0, one launch (start us, length us, event | category | flops | bytes accessed | tf_op | source)
XLA Modules:
  0.0 3162.6 jit_solution(10102721231775856310)
XLA Ops:
  19.4 30.5 all-to-all-done.4
  51.0 51.7 %all-gather.16.cloned.1.call-done = bf16[2048,2048]{1,0:T(8,128)(2,1)} async-done(((bf16[64,2048]{1,0:T(8,128)(2,1)}), bf16[2048,2048]{1,0:T(8,128)(2,1)}) %all-gather.16.cloned.1.call-update) | async-done | bytes 8388624 | tf_op jit(solution)/shard_map/all_gather | solution.py:192
  114.5 11.6 reduce.32
  134.0 58.4 %all-gather.14.cloned.1.call-done = bf16[2048,2048]{1,0:T(8,128)(2,1)} async-done(((bf16[64,2048]{1,0:T(8,128)(2,1)}), bf16[2048,2048]{1,0:T(8,128)(2,1)}) %all-gather.14.cloned.1.call-update) | async-done | bytes 8388624 | tf_op jit(solution)/shard_map/all_gather | solution.py:191
  201.6 69.9 %all-gather.12.cloned.1.call-done = bf16[2048,2048]{1,0:T(8,128)(2,1)} async-done(((bf16[64,2048]{1,0:T(8,128)(2,1)}), bf16[2048,2048]{1,0:T(8,128)(2,1)}) %all-gather.12.cloned.1.call-update) | async-done | bytes 8388624 | tf_op jit(solution)/shard_map/all_gather | solution.py:190
  292.6 11.6 reduce.31
  313.6 10.6 reduce.30
  325.9 32.3 %all-to-all-done.1 = bf16[4,2,65536]{2,1,0:T(2,128)(2,1)} async-done(((bf16[4,2,65536]{2,1,0:T(2,128)(2,1)}), bf16[4,2,65536]{2,1,0:T(2,128)(2,1)}, u32[]{:S(2)}, u32[]{:S(2)}) %all-to-all-start.1) | async-done | bytes 1048608 | tf_op jit(solution)/shard_map/all_to_all | solution.py:205
  372.1 14.9 all-to-all-done
  399.5 25.0 while.27
  431.6 9.0 reduce.33
  444.4 28.8 all_to_all.204
  485.8 55.2 %all_to_all.205 = bf16[64,4,2048]{2,0,1:T(8,128)(2,1)} all-to-all(bf16[64,4,2048]{2,0,1:T(8,128)(2,1)S(1)} %bitcast.465), channel_id=1, replica_groups=mesh['dp'=8,'seq'=4] {'seq'}, dimensions={1} | all-to-all | bytes 2097152 | tf_op jit(solution)/shard_map/all_to_all | solution.py:217
  541.2 52.8 %all_to_all.206 = bf16[64,4,2048]{2,0,1:T(8,128)(2,1)} all-to-all(bf16[64,4,2048]{2,0,1:T(8,128)(2,1)S(1)} %bitcast.466), channel_id=1, replica_groups=mesh['dp'=8,'seq'=4] {'seq'}, dimensions={1} | all-to-all | bytes 2097152 | tf_op jit(solution)/shard_map/all_to_all | solution.py:218
  594.1 9.8 all-gather.20.cloned.1.call-done
  604.0 14.6 fusion.50
  618.5 39.9 %all-gather.24.cloned.1.call-done = bf16[2048,2048]{1,0:T(8,128)(2,1)} async-done(((bf16[256,2048]{1,0:T(8,128)(2,1)}), bf16[2048,2048]{1,0:T(8,128)(2,1)}) %all-gather.24.cloned.1.call-update) | async-done | bytes 8388624 | tf_op jit(solution)/shard_map/all_gather | solution.py:222
  658.4 16.9 multiply_convert_fusion.2
  675.3 39.4 %all-gather.26.cloned.1.call-done = bf16[2048,2048]{1,0:T(8,128)(2,1)} async-done(((bf16[256,2048]{1,0:T(8,128)(2,1)}), bf16[2048,2048]{1,0:T(8,128)(2,1)}) %all-gather.26.cloned.1.call-update) | async-done | bytes 8388624 | tf_op jit(solution)/shard_map/all_gather | solution.py:223
  714.8 13.9 convolution_convert_fusion.3
  729.3 286.3 %all-gather.30.cloned.1.call-done = bf16[4096,2048]{1,0:T(8,128)(2,1)} async-done(((bf16[1024,2048]{1,0:T(8,128)(2,1)}), bf16[4096,2048]{1,0:T(8,128)(2,1)}) %all-gather.30.cloned.1.call-update) | async-done | bytes 16777232 | tf_op jit(solution)/shard_map/all_gather | solution.py:233
  1015.6 12.9 reduce.29
  1031.6 64.4 %all-gather.28.cloned.1.call-done = bf16[1,1024,2048]{2,1,0:T(8,128)(2,1)} async-done(((bf16[1,256,2048]{2,1,0:T(8,128)(2,1)}), bf16[1,1024,2048]{2,1,0:T(8,128)(2,1)}) %all-gather.28.cloned.1.call-update) | async-done | bytes 4194320 | tf_op jit(solution)/shard_map/all_gather | solution.py:227
  1101.1 23.0 multiply_convert_fusion.1
  1124.1 12.7 fusion.93
  1136.8 13.6 add_bitcast_fusion
  1150.5 14.5 convolution_convert_fusion.1
  1165.0 11.2 convolution_convert_fusion.2
  1176.2 13.5 convolution_convert_fusion
  1189.8 18.1 pad_maximum_fusion.1
  1215.2 78.4 %reduce-scatter.9.cloned.1.call-done = f32[1,256,2048]{2,1,0:T(8,128)} async-done(((f32[1,1024,2048]{2,1,0:T(8,128)}), f32[1,256,2048]{2,1,0:T(8,128)}) %reduce-scatter.9.cloned.1.call-update) | async-done | bytes 2097168 | tf_op jit(solution)/shard_map/reduce_scatter | solution.py:248
  1310.0 10.8 reduce.34
  1327.3 25.4 all-to-all-done.7
  1363.5 43.5 %while.28 = (s32[]{:T(128)}, f32[1,1024,4,128]{1,3,2,0:T(8,128)S(1)}, f32[1,1024,4,128]{1,3,2,0:T(8,128)}, bf16[2,1,512,4,128]{4,3,2,0,1:T(4,128)(2,1)}, s32[2]{...) while((s32[]{:T(128)}, ...), condition=%wide.region_15.16_spmd.clone, body=%wide.region_13.15_spmd.clone.sunk | while | flops 2720528896 | bytes 98113936 | solution.py:150
  1439.9 14.2 all-to-all-done.8
  1462.1 8.1 reduce.35
  1474.1 9.8 all-to-all-done.9
  1487.4 8.2 fusion.94
  1538.7 8.1 convolution_bitcast_fusion.2
  1546.8 8.2 convolution_bitcast_fusion.1
  1555.1 8.1 convolution_bitcast_fusion
  1563.3 45.0 %pad_maximum_fusion = f32[2048,8192]{0,1:T(8,128)} fusion(f32[2048,2048]{0,1:T(8,128)} %fusion.94, f32[2048,2048]{0,1:T(8,128)} %convolution_bitcast_fusion, f32[2048,2048]{0,1:T(8,128)} %convolution_bitcast_fusion.1, f32[2048,2048]{0,1:T(8,128)} %convolution_bitcast_fusion.2), kind=kLoop, calls=%fused_computation.57 | loop fusion | flops 50331648 | bytes 134217728 | tf_op jit(solution)/shard_map/concatenate | solution.py:321
  1608.3 61.2 %copy.230 = f32[2048,8192]{1,0:T(8,128)} copy(f32[2048,8192]{0,1:T(8,128)} %pad_maximum_fusion) | data formatting | bytes 134217728
  1681.5 24.2 all-to-all-done.13
  1727.6 36.1 %all-to-all-done.12 = bf16[4,64,2048]{2,1,0:T(8,128)(2,1)} async-done(((bf16[4,64,2048]{2,1,0:T(8,128)(2,1)}), bf16[4,64,2048]{2,1,0:T(8,128)(2,1)}, u32[]{:S(2)}, u32[]{:S(2)}) %all-to-all-start.12) | async-done | bytes 1048608 | tf_op jit(solution)/shard_map/all_to_all | solution.py:276
  1768.0 8.5 fusion.55
  1785.6 34.6 %all-to-all-done.11 = bf16[4,64,2048]{2,1,0:T(8,128)(2,1)} async-done(((bf16[4,64,2048]{2,1,0:T(8,128)(2,1)}), bf16[4,64,2048]{2,1,0:T(8,128)(2,1)}, u32[]{:S(2)}, u32[]{:S(2)}) %all-to-all-start.11) | async-done | bytes 1048608 | tf_op jit(solution)/shard_map/all_to_all | solution.py:269
  1823.1 1329.7 %reduce-scatter.13.cloned.1.call-done = f32[64,8192]{1,0:T(8,128)} async-done(((f32[2048,8192]{1,0:T(8,128)}), f32[64,8192]{1,0:T(8,128)}) %reduce-scatter.13.cloned.1.call-update) | async-done | bytes 2097168
  (385 shorter events, 375.6 us)
Async XLA Ops:
  7.2 95.5 %copy-start.15 = (bf16[1,256,2048]{2,1,0:T(8,128)(2,1)S(1)}, bf16[1,256,2048]{2,1,0:T(8,128)(2,1)}, u32[]{:S(2)}) copy-start(bf16[1,256,2048]{2,1,0:T(8,128)(2,1)} %param.18) | copy-start | bytes 3145732
  7.2 95.5 %all-gather.16.cloned.1.call-start = ((), (), s32[]{:S(2)}) async-start(), calls=%async_computation.20 | async-start | bytes 8650752 | tf_op jit(solution)/shard_map/all_gather | solution.py:192
  7.9 184.5 %all-gather.14.cloned.1.call-start = ((), (), s32[]{:S(2)}) async-start(), calls=%async_computation.19 | async-start | bytes 8650752 | tf_op jit(solution)/shard_map/all_gather | solution.py:191
  8.7 262.8 %all-gather.12.cloned.1.call-start = ((), (), s32[]{:S(2)}) async-start(), calls=%async_computation.18 | async-start | bytes 8650752 | tf_op jit(solution)/shard_map/all_gather | solution.py:190
  9.4 467.3 %all-gather.18.cloned.1.call-start = ((), (), s32[]{:S(2)}) async-start(), calls=%async_computation.21 | async-start | bytes 8650752 | tf_op jit(solution)/shard_map/all_gather | solution.py:193
  12.3 37.6 %all-to-all-start.4 = ((bf16[64,4,2048]{2,0,1:T(8,128)(2,1)}), bf16[64,4,2048]{2,0,1:T(8,128)(2,1)S(1)}, u32[]{:S(2)}, u32[]{:S(2)}) async-start(bf16[64,4,2048]{2,0,1:T(8,128)(2,1)} %bitcast.366), calls=%async_computation.4 | async-start | bytes 2097152 | tf_op jit(solution)/shard_map/all_to_all | solution.py:216
  18.6 575.5 %all-gather.22.cloned.1.call-start = ((), (), s32[]{:S(2)}) async-start(), calls=%async_computation.23 | async-start | bytes 9437184 | tf_op jit(solution)/shard_map/all_gather | solution.py:221
  19.2 83.5 %copy-start.42 = (f32[256,128]{0,1:T(8,128)}, f32[256,128]{0,1:T(8,128)S(1)}, u32[]{:S(2)}) copy-start(f32[256,128]{0,1:T(8,128)S(1)} %get-tuple-element.402) | copy-start | bytes 393220
  19.2 83.5 %copy-start.44 = (f32[256,128]{0,1:T(8,128)}, f32[256,128]{0,1:T(8,128)S(1)}, u32[]{:S(2)}) copy-start(f32[256,128]{0,1:T(8,128)S(1)} %get-tuple-element.403) | copy-start | bytes 393220
  129.5 178.2 %all-to-all-start.2 = ((bf16[4,2,65536]{2,1,0:T(2,128)(2,1)}), bf16[4,2,65536]{2,1,0:T(2,128)(2,1)}, u32[]{:S(2)}, u32[]{:S(2)}) async-start(bf16[4,2,65536]{2,1,0:T(2,128)(2,1)} %reshape.926), calls=%async_computation.2 | async-start | bytes 2097152 | tf_op jit(solution)/shard_map/all_to_all | solution.py:206
  134.0 64.3 %copy-start.52 = (f32[2048]{0:T(1024)S(1)}, f32[2048]{0:T(1024)}, u32[]{:S(2)}) copy-start(f32[2048]{0:T(1024)} %param.28) | copy-start | bytes 24580
  198.2 84.3 %copy-start.8 = (f32[256,2048]{1,0:T(8,128)}, f32[256,2048]{1,0:T(8,128)S(1)}, u32[]{:S(2)}) copy-start(f32[256,2048]{1,0:T(8,128)S(1)} %get-tuple-element.411) | copy-start | bytes 6291460
  198.2 84.3 %copy-start.61 = (f32[256]{0:T(256)}, f32[256]{0:T(256)S(1)}, u32[]{:S(2)}) copy-start(f32[256]{0:T(256)S(1)} %fusion.85) | copy-start | bytes 3076
  201.6 75.7 %copy-start.54 = (f32[2048]{0:T(1024)S(1)}, f32[2048]{0:T(1024)}, u32[]{:S(2)}) copy-start(f32[2048]{0:T(1024)} %param.27) | copy-start | bytes 24580
  307.7 50.5 %all-to-all-start.1 = ((bf16[4,2,65536]{2,1,0:T(2,128)(2,1)}), bf16[4,2,65536]{2,1,0:T(2,128)(2,1)}, u32[]{:S(2)}, u32[]{:S(2)}) async-start(bf16[4,2,65536]{2,1,0:T(2,128)(2,1)} %reshape.924), calls=%async_computation.1 | async-start | bytes 2097152 | tf_op jit(solution)/shard_map/all_to_all | solution.py:205
  358.1 28.8 all-to-all-start
  362.4 241.5 %all-gather.20.cloned.1.call-start = ((), (), s32[]{:S(2)}) async-start(), calls=%async_computation.22 | async-start | bytes 5242880 | tf_op jit(solution)/shard_map/all_gather | solution.py:226
  424.4 19.9 copy-start
  424.4 19.9 copy-start.2
  424.4 19.9 copy-start.6
  424.4 20.0 copy-start.56
  485.7 55.5 %copy-start.47 = (bf16[8192,64]{0,1:T(8,128)(2,1)S(1)}, bf16[8192,64]{0,1:T(8,128)(2,1)}, u32[]{:S(2)}) copy-start(bf16[8192,64]{0,1:T(8,128)(2,1)} %param.26) | copy-start | bytes 3145732
  485.7 172.8 %all-gather.24.cloned.1.call-start = ((), (), s32[]{:S(2)}) async-start(), calls=%async_computation.24 | async-start | bytes 9437184 | tf_op jit(solution)/shard_map/all_gather | solution.py:222
  541.1 173.7 %all-gather.26.cloned.1.call-start = ((), (), s32[]{:S(2)}) async-start(), calls=%async_computation.25 | async-start | bytes 9437184 | tf_op jit(solution)/shard_map/all_gather | solution.py:223
  594.0 421.6 %all-gather.30.cloned.1.call-start = ((), (), s32[]{:S(2)}) async-start(), calls=%async_computation.29 | async-start | bytes 20971520 | tf_op jit(solution)/shard_map/all_gather | solution.py:233
  728.7 367.3 %all-gather.28.cloned.1.call-start = ((), (), s32[]{:S(2)}) async-start(), calls=%async_computation.26 | async-start | bytes 5242880 | tf_op jit(solution)/shard_map/all_gather | solution.py:227
  729.3 564.3 %reduce-scatter.9.cloned.1.call-start = ((), (), s32[]{:S(2)}) async-start(), calls=%async_computation.27 | async-start | bytes 10485760 | tf_op jit(solution)/shard_map/reduce_scatter | solution.py:248
  1028.6 67.5 %copy-start.58 = (f32[2048]{0:T(1024)S(1)}, f32[2048]{0:T(1024)}, u32[]{:S(2)}) copy-start(f32[2048]{0:T(1024)} %param.30) | copy-start | bytes 24580
  1150.4 519.1 %reduce-scatter.11.cloned.1.call-start = ((), (), s32[]{:S(2)}) async-start(), calls=%async_computation.28 | async-start | bytes 28311552 | tf_op jit(solution)/shard_map/reduce_scatter | solution.py:255
  1150.5 14.5 copy-start.73
  1207.9 85.7 %copy-start.14 = (f32[256,2048]{1,0:T(8,128)S(1)}, f32[256,2048]{1,0:T(8,128)}, u32[]{:S(2)}) copy-start(f32[256,2048]{1,0:T(8,128)} %copy-done.13) | copy-start | bytes 6291460
  1207.9 85.7 %copy-start.17 = (bf16[1,256,2048]{2,1,0:T(8,128)(2,1)S(1)}, bf16[1,256,2048]{2,1,0:T(8,128)(2,1)}, u32[]{:S(2)}) copy-start(bf16[1,256,2048]{2,1,0:T(8,128)(2,1)} %param.18) | copy-start | bytes 3145732
  1207.9 85.7 %copy-start.51 = (f32[2048]{0:T(1024)S(1)}, f32[2048]{0:T(1024)}, u32[]{:S(2)}) copy-start(f32[2048]{0:T(1024)} %param.29) | copy-start | bytes 24580
  1207.9 85.7 %copy-start.66 = (f32[256]{0:T(256)S(1)}, f32[256]{0:T(256)}, u32[]{:S(2)}) copy-start(f32[256]{0:T(256)} %copy-done.65) | copy-start | bytes 3076
  1215.2 84.8 %copy-start.68 = (f32[256]{0:T(256)S(1)}, f32[256]{0:T(256)}, u32[]{:S(2)}) copy-start(f32[256]{0:T(256)} %copy-done.67) | copy-start | bytes 3076
  1322.5 30.2 all-to-all-start.7
  1424.2 29.9 all-to-all-start.8
  1454.1 29.7 all-to-all-start.9
  1462.1 25.3 copy-start.24
  1470.2 17.2 copy-start.41
  1483.8 28.7 all-to-all-start.10
  1487.3 289.1 %reduce-scatter.15.cloned.1.call-start = ((), (), s32[]{:S(2)}) async-start(), calls=%async_computation.31 | async-start | bytes 1081344
  1563.2 1589.6 %reduce-scatter.13.cloned.1.call-start = ((), (), s32[]{:S(2)}) async-start(), calls=%async_computation.30 | async-start | bytes 69206016
  1674.4 31.4 all-to-all-start.13
  1705.8 57.9 %all-to-all-start.12 = ((bf16[4,64,2048]{2,1,0:T(8,128)(2,1)}), bf16[4,64,2048]{2,1,0:T(8,128)(2,1)}, u32[]{:S(2)}, u32[]{:S(2)}) async-start(bf16[4,64,2048]{2,1,0:T(8,128)(2,1)} %bitcast.463), calls=%async_computation.14 | async-start | bytes 2097152 | tf_op jit(solution)/shard_map/all_to_all | solution.py:276
  1725.1 42.8 %copy-start.26 = (bf16[1,256,2048]{2,1,0:T(8,128)(2,1)S(1)}, bf16[1,256,2048]{2,1,0:T(8,128)(2,1)}, u32[]{:S(2)}) copy-start(bf16[1,256,2048]{2,1,0:T(8,128)(2,1)} %param.31) | copy-start | bytes 3145732
  1725.1 42.8 %copy-start.28 = (f32[1,256,2048]{2,1,0:T(8,128)S(1)}, f32[1,256,2048]{2,1,0:T(8,128)}, u32[]{:S(2)}) copy-start(f32[1,256,2048]{2,1,0:T(8,128)} %reduce-scatter.9.cloned.1.call-done) | copy-start | bytes 6291460
  1763.7 56.5 %all-to-all-start.11 = ((bf16[4,64,2048]{2,1,0:T(8,128)(2,1)}), bf16[4,64,2048]{2,1,0:T(8,128)(2,1)}, u32[]{:S(2)}, u32[]{:S(2)}) async-start(bf16[4,64,2048]{2,1,0:T(8,128)(2,1)} %bitcast.460), calls=%async_computation.13 | async-start | bytes 2097152 | tf_op jit(solution)/shard_map/all_to_all | solution.py:269
  (60 other events, 282.6 us)
Sparse Core Ops, SparseCore 0:
  11.0 91.6 all-gather.15
  105.6 86.7 all-gather.13
  195.3 76.0 all-gather.11
  274.3 89.3 all-gather.17
  365.4 52.4 all-gather.21
  485.8 118.1 all-gather.19
  605.8 52.5 all-gather.23
  660.3 54.3 all-gather.25
  728.8 286.7 all-gather.29
  1017.0 78.9 all-gather.27
  1150.6 142.9 reduce-scatter.8
  1297.1 157.6 reduce-scatter.10
  1563.3 138.2 reduce-scatter.14
  1703.9 1448.8 reduce-scatter.12
